TPU v7x, 32 devices: a whole 2x2x4 slice. The times are simulated.
32 devices in a mesh: ctx: 8 (over z, x), head: 4 (over y, core).
Axes of the slice: x: 2, y: 2, z: 4, core: 2. Of those that a mesh axis runs over, the one named last changes fastest.
Arguments:
- query_rows: bfloat16 [8192, 6144], P(('ctx', 'head')), may hold values from -0.52734375 to 0.52734375
- key_rows: bfloat16 [8192, 6144], P(('ctx', 'head')), may hold values from -0.52734375 to 0.52734375
- value_rows: bfloat16 [8192, 6144], P(('ctx', 'head')), may hold values from -0.62890625 to 0.62890625
- grad_out: bfloat16 [8192, 6144], P(('ctx', 'head')), may hold values from -0.62890625 to 0.62890625
- decay_rates: float32 [48], replicated, as said below
Outputs:
- query_gradient: bfloat16 [8192, 6144], P(('ctx', 'head'))
- grad_key: bfloat16 [8192, 6144], P(('ctx', 'head'))
- value_gradient: bfloat16 [8192, 6144], P(('ctx', 'head'))
Inputs may be any that keep to these rules, and one draw needn't show every extreme that they name: decay_rates lie between 0.1 / 8192 and 24 / 256.
All inputs are finite; a program needn't handle non-finite values.
Results may differ from a plain program's by a relative error of at most 0.0056.
Values may be sent and summed in bfloat16 or wider, within the bound.
No kernel may reach another device: no remote copies, remote signals or barrier semaphores. Data moves between devices by JAX's collectives and lax.ppermute only.
A program may use at most 128 MiB of HBM per device.

v0:
```python
import jax
import jax.numpy as jnp
from jax import lax
from jax.sharding import PartitionSpec as P

DH = 128
BLOCK = 256
HIGHEST = lax.Precision.HIGHEST


def carried_in(value, axis, join, neutral, backward):
    count, mine = (lax.axis_size(axis), lax.axis_index(axis))
    pieces = jax.tree.map(lambda part: lax.all_gather(part, axis), value)
    if backward:
        pieces = jax.tree.map(lambda part: part[::-1], pieces)
        mine = count - 1 - mine
    subtotal = jax.tree.map(
        lambda part, zero: jnp.full_like(part, 0) + jnp.asarray(zero, part.dtype), value, neutral
    )

    def lap(position, subtotal):
        longer = join(subtotal, jax.tree.map(lambda part: part[position], pieces))
        return jax.tree.map(lambda new, old: jnp.where(position < mine, new, old), longer, subtotal)

    return lax.fori_loop(0, count - 1, lap, subtotal)


def combine_states(earlier, later):
    decay_early, state_early = earlier
    decay_late, state_late = later
    return (decay_early * decay_late, decay_late[:, None, None] * state_early + state_late)


def local(query_rows, key_rows, value_rows, grad_out, decay_rates):
    queries, keys_here, values, grads = (
        lax.all_to_all(query_rows, "head", split_axis=1, concat_axis=0, tiled=True),
        lax.all_to_all(key_rows, "head", split_axis=1, concat_axis=0, tiled=True),
        lax.all_to_all(value_rows, "head", split_axis=1, concat_axis=0, tiled=True),
        lax.all_to_all(grad_out, "head", split_axis=1, concat_axis=0, tiled=True),
    )
    rows = queries.shape[0]
    heads_here = queries.shape[1] // DH
    nblocks = rows // BLOCK
    rates = lax.dynamic_slice_in_dim(
        decay_rates, lax.axis_index("head") * heads_here, heads_here, 0
    )
    shape_four = (nblocks, BLOCK, heads_here, DH)
    q_blocks = queries.reshape(shape_four)
    key_block_list = keys_here.reshape(shape_four)
    v_blocks = values.reshape(shape_four)
    gradient_block_list = grads.reshape(shape_four)
    position = jnp.arange(BLOCK, dtype=jnp.float32)
    offset = position[:, None] - position[None, :]
    decay_mask = jnp.where(
        offset[None] >= 0.0, jnp.exp(-rates[:, None, None] * jnp.maximum(offset, 0.0)[None]), 0.0
    )
    grad_scores = jnp.einsum(
        "nihd,njhd->nhij", gradient_block_list, v_blocks, preferred_element_type=jnp.float32
    )
    weight_gradient_set = (grad_scores * decay_mask[None]).astype(jnp.bfloat16)
    fwd_scores = jnp.einsum(
        "nihd,njhd->nhij", q_blocks, key_block_list, preferred_element_type=jnp.float32
    )
    forward_weight_set = (fwd_scores * decay_mask[None]).astype(jnp.bfloat16)
    key_decay = jnp.exp(-rates[None, :] * (BLOCK - 1.0 - position)[:, None])
    query_decay = jnp.exp(-rates[None, :] * position[:, None])
    keys_decayed = (key_block_list * key_decay[None, :, :, None]).astype(jnp.bfloat16)
    decayed_query_rows = (q_blocks * query_decay[None, :, :, None]).astype(jnp.bfloat16)
    block_kv = jnp.einsum(
        "njhd,njhe->nhde", keys_decayed, v_blocks, preferred_element_type=jnp.float32
    )
    query_decay_block = jnp.einsum(
        "nihd,nihe->nhde",
        decayed_query_rows,
        gradient_block_list,
        preferred_element_type=jnp.float32,
    )
    block_index = jnp.arange(nblocks, dtype=jnp.float32)
    block_gap = block_index[:, None] - block_index[None, :]
    fwd_inside = jnp.where(
        block_gap[None] >= 1.0,
        jnp.exp(-rates[:, None, None] * BLOCK * jnp.maximum(block_gap - 1.0, 0.0)[None]),
        0.0,
    )
    rev_inside = jnp.where(
        block_gap[None] <= -1.0,
        jnp.exp(-rates[:, None, None] * BLOCK * jnp.maximum(-block_gap - 1.0, 0.0)[None]),
        0.0,
    )
    start_power = jnp.exp(-rates[:, None] * BLOCK * block_index[None, :])
    end_power = jnp.exp(-rates[:, None] * BLOCK * (nblocks - 1.0 - block_index)[None, :])
    local_fwd = jnp.einsum("hm,mhde->hde", end_power, block_kv, precision=HIGHEST)
    local_rev = jnp.einsum("hm,mhde->hde", start_power, query_decay_block, precision=HIGHEST)
    device_span = jnp.exp(-rates * rows)
    identity = (jnp.ones((heads_here,), jnp.float32), jnp.zeros((heads_here, DH, DH), jnp.float32))
    before_device = carried_in((device_span, local_fwd), "ctx", combine_states, identity, False)[1]
    after_device = carried_in((device_span, local_rev), "ctx", combine_states, identity, True)[1]
    state_before = jnp.einsum(
        "hnm,mhde->nhde", fwd_inside, block_kv, precision=HIGHEST
    ) + jnp.einsum("hn,hde->nhde", start_power, before_device, precision=HIGHEST)
    state_after = jnp.einsum(
        "hnm,mhde->nhde", rev_inside, query_decay_block, precision=HIGHEST
    ) + jnp.einsum("hn,hde->nhde", end_power, after_device, precision=HIGHEST)
    state_before_bfloat = state_before.astype(jnp.bfloat16)
    state_after_bfloat = state_after.astype(jnp.bfloat16)
    leading_part = jnp.exp(-rates[None, :] * (position + 1.0)[:, None])[None, :, :, None]
    trailing_part = jnp.exp(-rates[None, :] * (BLOCK - position)[:, None])[None, :, :, None]
    query_gradient = jnp.einsum(
        "nhij,njhd->nihd", weight_gradient_set, key_block_list, preferred_element_type=jnp.float32
    ) + leading_part * jnp.einsum(
        "nihe,nhde->nihd",
        gradient_block_list,
        state_before_bfloat,
        preferred_element_type=jnp.float32,
    )
    grad_key = jnp.einsum(
        "nhij,nihd->njhd", weight_gradient_set, q_blocks, preferred_element_type=jnp.float32
    ) + trailing_part * jnp.einsum(
        "njhe,nhde->njhd", v_blocks, state_after_bfloat, preferred_element_type=jnp.float32
    )
    value_gradient = jnp.einsum(
        "nhij,nihe->njhe",
        forward_weight_set,
        gradient_block_list,
        preferred_element_type=jnp.float32,
    ) + trailing_part * jnp.einsum(
        "njhd,nhde->njhe", key_block_list, state_after_bfloat, preferred_element_type=jnp.float32
    )
    flat_shape = (rows, heads_here * DH)
    return (
        lax.all_to_all(
            query_gradient.reshape(flat_shape).astype(jnp.bfloat16),
            "head",
            split_axis=0,
            concat_axis=1,
            tiled=True,
        ),
        lax.all_to_all(
            grad_key.reshape(flat_shape).astype(jnp.bfloat16),
            "head",
            split_axis=0,
            concat_axis=1,
            tiled=True,
        ),
        lax.all_to_all(
            value_gradient.reshape(flat_shape).astype(jnp.bfloat16),
            "head",
            split_axis=0,
            concat_axis=1,
            tiled=True,
        ),
    )


def solution(mesh):
    return jax.shard_map(
        local,
        mesh=mesh,
        in_specs=(
            P(("ctx", "head"), None),
            P(("ctx", "head"), None),
            P(("ctx", "head"), None),
            P(("ctx", "head"), None),
            P(),
        ),
        out_specs=(P(("ctx", "head"), None), P(("ctx", "head"), None), P(("ctx", "head"), None)),
        check_vma=False,
    )
```

profile of v0, /device:TPU:0, one launch (start us, length us, event | category | flops | bytes accessed | tf_op | source)
XLA Modules:
  0.0 421.6 jit_solution(8418679412917657691)
XLA Ops:
  7.2 4.6 %copy.37 = bf16[256,6144]{0,1:T(8,128)(2,1)} copy(bf16[256,6144]{1,0:T(8,128)(2,1)} %param.12) | data formatting | bytes 6291456 | tf_op args[3]
  11.8 4.3 %all-to-all-start = ((bf16[256,4,1536]{0,2,1:T(8,128)(2,1)}), bf16[256,4,1536]{0,2,1:T(8,128)(2,1)S(1)}, u32[]{:S(2)}, u32[]{:S(2)}) async-start(bf16[256,4,1536]{0,2,1:T(8,128)(2,1)} %bitcast.126), calls=%async_computation | async-start | bytes 6291456 | tf_op jit(solution)/shard_map/all_to_all | solution.py:39
  16.1 4.6 %copy.75 = bf16[256,6144]{0,1:T(8,128)(2,1)} copy(bf16[256,6144]{1,0:T(8,128)(2,1)} %param.9) | data formatting | bytes 6291456 | tf_op jit(solution)/shard_map/all_to_all | solution.py:36
  20.7 32.4 %all-to-all-done = bf16[256,4,1536]{0,2,1:T(8,128)(2,1)S(1)} async-done(((bf16[256,4,1536]{0,2,1:T(8,128)(2,1)}), bf16[256,4,1536]{0,2,1:T(8,128)(2,1)S(1)}, u32[]{:S(2)}, u32[]{:S(2)}) %all-to-all-start) | async-done | bytes 3145760 | tf_op jit(solution)/shard_map/all_to_all | solution.py:39
  53.1 4.8 %all-to-all-start.4 = ((bf16[256,4,1536]{0,2,1:T(8,128)(2,1)}), bf16[256,4,1536]{0,2,1:T(8,128)(2,1)}, u32[]{:S(2)}, u32[]{:S(2)}) async-start(bf16[256,4,1536]{0,2,1:T(8,128)(2,1)} %bitcast.123), calls=%async_computation.4 | async-start | bytes 6291456 | tf_op jit(solution)/shard_map/all_to_all | solution.py:36
  57.9 0.6 dynamic-slice
  59.2 0.2 exponential_dynamic-update-slice_fusion
  59.4 0.1 fusion.55
  59.5 0.1 multiply_exponential_fusion
  59.6 35.2 %all-to-all-done.4 = bf16[256,4,1536]{0,2,1:T(8,128)(2,1)} async-done(((bf16[256,4,1536]{0,2,1:T(8,128)(2,1)}), bf16[256,4,1536]{0,2,1:T(8,128)(2,1)}, u32[]{:S(2)}, u32[]{:S(2)}) %all-to-all-start.4) | async-done | bytes 3145760 | tf_op jit(solution)/shard_map/all_to_all | solution.py:36
  94.8 2.9 fusion.13
  97.7 1.7 copy-done.4
  99.4 7.1 %fusion.16 = f32[12,1,128,128]{3,1,2,0:T(1,128)} fusion(f32[4,12,128,128]{3,2,1,0:T(8,128)S(1)} %fusion.13, f32[12,4,1,1]{1,0,2,3:T(8,128)S(1)} %get-tuple-element.253), kind=kOutput, calls=%fused_computation.29 | convolution fusion | flops 9437184 | bytes 3932352 | tf_op jit(solution)/shard_map/hm,mhde->hde/dot_general | solution.py:93
  106.5 4.6 %copy.38 = bf16[256,6144]{0,1:T(8,128)(2,1)} copy(bf16[256,6144]{1,0:T(8,128)(2,1)} %param.11) | data formatting | bytes 6291456 | tf_op args[2]
  111.1 4.7 %all-to-all-start.1 = ((bf16[256,4,1536]{0,2,1:T(8,128)(2,1)}), bf16[256,4,1536]{0,2,1:T(8,128)(2,1)}, u32[]{:S(2)}, u32[]{:S(2)}) async-start(bf16[256,4,1536]{0,2,1:T(8,128)(2,1)} %bitcast.125), calls=%async_computation.1 | async-start | bytes 6291456 | tf_op jit(solution)/shard_map/all_to_all | solution.py:38
  115.8 0.0 all-gather.6.cloned.1.call-start
  115.8 4.7 %copy.73 = bf16[256,6144]{0,1:T(8,128)(2,1)} copy(bf16[256,6144]{1,0:T(8,128)(2,1)} %param.10) | data formatting | bytes 6291456 | tf_op jit(solution)/shard_map/all_to_all | solution.py:37
  120.5 32.2 %all-to-all-done.1 = bf16[256,4,1536]{0,2,1:T(8,128)(2,1)} async-done(((bf16[256,4,1536]{0,2,1:T(8,128)(2,1)}), bf16[256,4,1536]{0,2,1:T(8,128)(2,1)}, u32[]{:S(2)}, u32[]{:S(2)}) %all-to-all-start.1) | async-done | bytes 3145760 | tf_op jit(solution)/shard_map/all_to_all | solution.py:38
  152.8 40.6 %all_to_all.112 = bf16[256,4,1536]{0,2,1:T(8,128)(2,1)S(1)} all-to-all(bf16[256,4,1536]{0,2,1:T(8,128)(2,1)} %bitcast.127), channel_id=1, replica_groups=mesh['ctx'=8,'head'=4] {'head'}, dimensions={1} | all-to-all | bytes 6291456 | tf_op jit(solution)/shard_map/all_to_all | solution.py:37
  193.3 4.0 fusion.12
  197.4 1.7 copy-done.3
  199.1 7.1 %fusion.20 = f32[12,1,128,128]{3,1,2,0:T(1,128)} fusion(f32[4,12,128,128]{3,2,1,0:T(8,128)S(1)} %fusion.12, f32[12,4,1,1]{1,0,2,3:T(8,128)S(1)} %get-tuple-element.255), kind=kOutput, calls=%fused_computation.33 | convolution fusion | flops 9437184 | bytes 3932352 | tf_op jit(solution)/shard_map/hm,mhde->hde/dot_general | solution.py:92
  206.2 23.3 %all-reduce = f32[96]{0:T(128)S(1)} all-reduce(f32[96]{0:T(128)S(1)} %get-tuple-element.249), channel_id=2, replica_groups=mesh['ctx'=8,'head'=4] {'ctx'}, use_global_device_ids=true, to_apply=%add | all-reduce | flops 96 | bytes 768
  229.5 0.1 reshape.266
  229.6 0.1 fusion.36
  229.7 0.1 fusion.35
  229.7 0.5 exponential_select_fusion
  230.3 4.9 %multiply_convert_fusion.1 = bf16[4,12,256,256]{3,2,1,0:T(8,128)(2,1)S(1)} fusion(f32[12,256,256]{2,1,0:T(8,128)S(1)} %exponential_select_fusion, bf16[4,256,12,128]{1,3,2,0:T(8,128)(2,1)S(1)} %bitcast.114, bf16[4,256,12,128]{1,3,2,0:T(8,128)(2,1)} %bitcast.5), kind=kOutput, calls=%fused_computation.7 | convolution fusion | flops 811597824 | bytes 15728640 | tf_op jit(solution)/shard_map/nihd,njhd->nhij/dot_general | solution.py:57
  235.2 2.6 copy-done.1
  237.8 5.5 %fusion.62 = f32[4,12,256,128]{2,3,1,0:T(8,128)} fusion(bf16[4,256,12,128]{1,3,2,0:T(8,128)(2,1)} %bitcast.27, bf16[4,12,256,256]{3,2,1,0:T(8,128)(2,1)S(1)} %multiply_convert_fusion.1), kind=kOutput, calls=%fused_computation.84 | convolution fusion | flops 805306368 | bytes 15728640 | tf_op jit(solution)/shard_map/nhij,nihd->njhd/dot_general | solution.py:116
  243.2 6.2 %rev.7 = f32[8,12,128,128]{3,2,1,0:T(8,128)} reverse(f32[8,12,128,128]{3,2,1,0:T(8,128)} %bitcast.129), dimensions={0} | reverse | bytes 12582912 | tf_op jit(solution)/shard_map/rev | solution.py:15
  249.5 16.9 %while.29 = (s32[]{:T(128)}, f32[12,128,128]{2,1,0:T(8,128)}, s32[]{:T(128)}, f32[8,12]{1,0:T(8,128)S(1)}, f32[8,12,128,128]{3,2,1,0:T(8,128)}, /*index=5*/s32[]{:T(128)}, s32[]{:T(128)}) while((s32[]{:T(128)}, f32[12,128,128]{2,1,0:T(8,128)}, s32[]{:T(128)}, f32[8,12]{1,0:T(8,128)S(1)}, f32[8,12,128,128]{3,2,1,0:T(8,128)}, ...), condition=%wide.region_3.4_spmd.clone, body=%wide.region_2.3_spmd.clone.sunk | while | flops 786436 | bytes 2359545 | solution.py:25
  249.5 2.4 fusion.82
  251.9 2.4 fusion.82
  254.3 2.4 fusion.82
  256.7 2.4 fusion.82
  259.2 2.4 fusion.82
  261.6 2.4 fusion.82
  264.0 2.4 fusion.82
  266.4 10.8 %fusion.32 = bf16[4,12,128,128]{3,0,2,1:T(4,128)(2,1)} fusion(f32[12,4]{1,0:T(8,128)S(1)} %get-tuple-element.256, f32[12,128,128]{2,1,0:T(8,128)} %get-tuple-element.192, f32[4,12,128,128]{3,2,1,0:T(8,128)} %copy-done.4, f32[4,4]{1,0:T(4,128)S(1)} %add_maximum_fusion, f32[12]{0:T(128)S(1)} %broadcast_multiply_fusion, pred[4,4]{1,0:T(4,128)(4,1)S(1)} %fusion.57), kind=kOutput, calls=%fused_computation.39 | convolution fusion | flops 40108416 | bytes 5505344 | tf_op jit(solution)/shard_map/hnm,mhde->nhde/dot_general | solution.py:101
  277.2 3.8 copy.55
  281.0 6.9 %fusion.6 = bf16[4,256,12,128]{1,3,2,0:T(8,128)(2,1)} fusion(f32[4,12,256,128]{2,3,1,0:T(8,128)} %fusion.62, f32[256,12]{0,1:T(8,128)S(1)} %get-tuple-element.258, bf16[4,12,128,128]{2,3,1,0:T(8,128)(2,1)} %copy.55, bf16[4,256,12,128]{1,3,2,0:T(8,128)(2,1)} %bitcast.5), kind=kOutput, calls=%fused_computation.14 | convolution fusion | flops 407371776 | bytes 14168064 | tf_op jit(solution)/shard_map/njhe,nhde->njhd/dot_general | solution.py:118
  287.9 4.9 %all-to-all-start.5 = ((bf16[4,256,1536]{1,2,0:T(8,128)(2,1)}), bf16[4,256,1536]{1,2,0:T(8,128)(2,1)}, u32[]{:S(2)}, u32[]{:S(2)}) async-start(bf16[4,256,1536]{1,2,0:T(8,128)(2,1)} %bitcast.128), calls=%async_computation.5 | async-start | bytes 6291456 | tf_op jit(solution)/shard_map/all_to_all | solution.py:138
  292.8 8.5 %fusion.61 = f32[4,12,256,128]{2,3,1,0:T(8,128)} fusion(bf16[4,12,256,256]{3,2,1,0:T(8,128)(2,1)} %copy-done.1, bf16[4,256,12,128]{1,3,2,0:T(8,128)(2,1)} %bitcast.118), kind=kOutput, calls=%fused_computation.83 | convolution fusion | flops 805306368 | bytes 15728640 | tf_op jit(solution)/shard_map/nhij,njhd->nihd/dot_general | solution.py:108
  301.3 9.1 %fusion.2 = f32[4,12,256,128]{2,3,1,0:T(8,128)} fusion(bf16[4,256,12,128]{1,3,2,0:T(8,128)(2,1)S(1)} %bitcast.115, f32[12,256,256]{2,1,0:T(8,128)} %copy-done.2, bf16[4,256,12,128]{1,3,2,0:T(8,128)(2,1)} %bitcast.27, bf16[4,256,12,128]{1,3,2,0:T(8,128)(2,1)} %bitcast.119), kind=kOutput, calls=%fused_computation.8 | convolution fusion | flops 1616904192 | bytes 18874368 | tf_op jit(solution)/shard_map/nhij,nihe->njhe/dot_general | solution.py:121
  310.4 6.9 %fusion.4 = bf16[4,256,12,128]{1,3,2,0:T(8,128)(2,1)} fusion(f32[4,12,256,128]{2,3,1,0:T(8,128)} %fusion.2, f32[256,12]{0,1:T(8,128)S(1)} %get-tuple-element.258, bf16[4,12,128,128]{2,3,1,0:T(8,128)(2,1)} %copy.55, bf16[4,256,12,128]{1,3,2,0:T(8,128)(2,1)} %bitcast.120), kind=kOutput, calls=%fused_computation.11 | convolution fusion | flops 407371776 | bytes 14168064 | tf_op jit(solution)/shard_map/njhd,nhde->njhe/dot_general | solution.py:126
  317.3 12.2 %all-to-all-done.5 = bf16[4,256,1536]{1,2,0:T(8,128)(2,1)} async-done(((bf16[4,256,1536]{1,2,0:T(8,128)(2,1)}), bf16[4,256,1536]{1,2,0:T(8,128)(2,1)}, u32[]{:S(2)}, u32[]{:S(2)}) %all-to-all-start.5) | async-done | bytes 3145760 | tf_op jit(solution)/shard_map/all_to_all | solution.py:138
  329.6 4.7 %all-to-all-start.6 = ((bf16[4,256,1536]{1,2,0:T(8,128)(2,1)}), bf16[4,256,1536]{1,2,0:T(8,128)(2,1)}, u32[]{:S(2)}, u32[]{:S(2)}) async-start(bf16[4,256,1536]{1,2,0:T(8,128)(2,1)} %bitcast.121), calls=%async_computation.6 | async-start | bytes 6291456 | tf_op jit(solution)/shard_map/all_to_all | solution.py:145
  334.2 16.9 %while.28 = (s32[]{:T(128)}, f32[12,128,128]{2,1,0:T(8,128)}, s32[]{:T(128)}, f32[8,12]{1,0:T(8,128)S(1)}, f32[8,12,128,128]{3,2,1,0:T(8,128)}, /*index=5*/s32[]{:T(128)}, s32[]{:T(128)}) while((s32[]{:T(128)}, f32[12,128,128]{2,1,0:T(8,128)}, s32[]{:T(128)}, f32[8,12]{1,0:T(8,128)S(1)}, f32[8,12,128,128]{3,2,1,0:T(8,128)}, ...), condition=%wide.region_1.2_spmd.clone, body=%wide.region_0.1_spmd.clone.sunk | while | flops 786436 | bytes 2359545 | solution.py:25
  334.3 2.2 fusion.81
  336.5 2.4 fusion.81
  338.9 2.4 fusion.81
  341.4 2.4 fusion.81
  343.8 2.4 fusion.81
  346.3 2.4 fusion.81
  348.7 2.4 fusion.81
  351.2 10.0 %fusion.29 = bf16[4,12,128,128]{3,0,2,1:T(4,128)(2,1)S(1)} fusion(f32[12,4]{1,0:T(8,128)S(1)} %get-tuple-element.254, f32[12,128,128]{2,1,0:T(8,128)} %get-tuple-element.191, f32[4,12,128,128]{3,2,1,0:T(8,128)} %copy-done.3, f32[4,4]{1,0:T(4,128)S(1)} %add_maximum_fusion.1, f32[12]{0:T(128)S(1)} %broadcast_multiply_fusion, pred[4,4]{1,0:T(4,128)(4,1)S(1)} %fusion.58), kind=kOutput, calls=%fused_computation.38 | convolution fusion | flops 40108416 | bytes 5505344 | tf_op jit(solution)/shard_map/hnm,mhde->nhde/dot_general | solution.py:98
  361.1 5.6 %fusion.8 = bf16[4,256,12,128]{1,3,2,0:T(8,128)(2,1)} fusion(f32[4,12,256,128]{2,3,1,0:T(8,128)} %fusion.61, f32[256,12]{0,1:T(8,128)S(1)} %get-tuple-element.260, bf16[4,256,12,128]{1,3,2,0:T(8,128)(2,1)S(1)} %bitcast.116, bf16[4,12,128,128]{3,0,2,1:T(4,128)(2,1)S(1)} %fusion.29), kind=kOutput, calls=%fused_computation.17 | convolution fusion | flops 407371776 | bytes 14168064 | tf_op jit(solution)/shard_map/nihe,nhde->nihd/dot_general | solution.py:110
  366.8 4.4 %all-to-all-done.6 = bf16[4,256,1536]{1,2,0:T(8,128)(2,1)} async-done(((bf16[4,256,1536]{1,2,0:T(8,128)(2,1)}), bf16[4,256,1536]{1,2,0:T(8,128)(2,1)}, u32[]{:S(2)}, u32[]{:S(2)}) %all-to-all-start.6) | async-done | bytes 3145760 | tf_op jit(solution)/shard_map/all_to_all | solution.py:145
  371.2 3.7 all-to-all-start.3
  374.9 4.6 %copy.76 = bf16[256,6144]{1,0:T(8,128)(2,1)} copy(bf16[256,6144]{0,1:T(8,128)(2,1)} %bitcast.40) | data formatting | bytes 6291456 | tf_op jit(solution)/shard_map/all_to_all | solution.py:138
  379.5 4.6 %copy.77 = bf16[256,6144]{1,0:T(8,128)(2,1)} copy(bf16[256,6144]{0,1:T(8,128)(2,1)} %bitcast.45) | data formatting | bytes 6291456 | tf_op jit(solution)/shard_map/all_to_all | solution.py:145
  384.2 27.6 %all-to-all-done.3 = bf16[4,256,1536]{1,2,0:T(8,128)(2,1)S(1)} async-done(((bf16[4,256,1536]{1,2,0:T(8,128)(2,1)}), bf16[4,256,1536]{1,2,0:T(8,128)(2,1)S(1)}, u32[]{:S(2)}, u32[]{:S(2)}) %all-to-all-start.3) | async-done | bytes 3145760 | tf_op jit(solution)/shard_map/all_to_all | solution.py:131
  411.8 3.0 copy.74
  (42 shorter events, 0.3 us)
Async XLA Ops:
  11.8 41.3 %all-to-all-start = ((bf16[256,4,1536]{0,2,1:T(8,128)(2,1)}), bf16[256,4,1536]{0,2,1:T(8,128)(2,1)S(1)}, u32[]{:S(2)}, u32[]{:S(2)}) async-start(bf16[256,4,1536]{0,2,1:T(8,128)(2,1)} %bitcast.126), calls=%async_computation | async-start | bytes 6291456 | tf_op jit(solution)/shard_map/all_to_all | solution.py:39
  53.1 4.9 %copy-start.6 = (u32[32]{0:T(128)S(1)}, u32[32]{0:T(128)}, u32[]{:S(2)}) copy-start(u32[32]{0:T(128)} %constant.87) | copy-start | bytes 388
  53.1 6.1 %copy-start.5 = (f32[48]{0:T(128)S(1)}, f32[48]{0:T(128)}, u32[]{:S(2)}) copy-start(f32[48]{0:T(128)} %param.13) | copy-start | bytes 580
  53.1 41.8 %all-to-all-start.4 = ((bf16[256,4,1536]{0,2,1:T(8,128)(2,1)}), bf16[256,4,1536]{0,2,1:T(8,128)(2,1)}, u32[]{:S(2)}, u32[]{:S(2)}) async-start(bf16[256,4,1536]{0,2,1:T(8,128)(2,1)} %bitcast.123), calls=%async_computation.4 | async-start | bytes 6291456 | tf_op jit(solution)/shard_map/all_to_all | solution.py:36
  57.9 185.4 %all-gather.8.cloned.1.call-start = ((), (), s32[]{:S(2)}) async-start(), calls=%async_computation.8 | async-start | bytes 7077888 | tf_op jit(solution)/shard_map/all_gather | solution.py:13
  97.7 1.7 copy-start.4
  111.1 41.6 %all-to-all-start.1 = ((bf16[256,4,1536]{0,2,1:T(8,128)(2,1)}), bf16[256,4,1536]{0,2,1:T(8,128)(2,1)}, u32[]{:S(2)}, u32[]{:S(2)}) async-start(bf16[256,4,1536]{0,2,1:T(8,128)(2,1)} %bitcast.125), calls=%async_computation.1 | async-start | bytes 6291456 | tf_op jit(solution)/shard_map/all_to_all | solution.py:38
  115.8 218.4 %all-gather.6.cloned.1.call-start = ((), (), s32[]{:S(2)}) async-start(), calls=%async_computation.7 | async-start | bytes 7077888 | tf_op jit(solution)/shard_map/all_gather | solution.py:13
  193.3 4.1 copy-start
  197.4 1.7 copy-start.3
  230.2 4.9 %copy-start.2 = (f32[12,256,256]{2,1,0:T(8,128)}, f32[12,256,256]{2,1,0:T(8,128)S(1)}, u32[]{:S(2)}) copy-start(f32[12,256,256]{2,1,0:T(8,128)S(1)} %exponential_select_fusion) | copy-start | bytes 9437188
  235.1 2.6 copy-start.1
  287.9 41.6 %all-to-all-start.5 = ((bf16[4,256,1536]{1,2,0:T(8,128)(2,1)}), bf16[4,256,1536]{1,2,0:T(8,128)(2,1)}, u32[]{:S(2)}, u32[]{:S(2)}) async-start(bf16[4,256,1536]{1,2,0:T(8,128)(2,1)} %bitcast.128), calls=%async_computation.5 | async-start | bytes 6291456 | tf_op jit(solution)/shard_map/all_to_all | solution.py:138
  329.6 41.6 %all-to-all-start.6 = ((bf16[4,256,1536]{1,2,0:T(8,128)(2,1)}), bf16[4,256,1536]{1,2,0:T(8,128)(2,1)}, u32[]{:S(2)}, u32[]{:S(2)}) async-start(bf16[4,256,1536]{1,2,0:T(8,128)(2,1)} %bitcast.121), calls=%async_computation.6 | async-start | bytes 6291456 | tf_op jit(solution)/shard_map/all_to_all | solution.py:145
  371.2 40.6 %all-to-all-start.3 = ((bf16[4,256,1536]{1,2,0:T(8,128)(2,1)}), bf16[4,256,1536]{1,2,0:T(8,128)(2,1)S(1)}, u32[]{:S(2)}, u32[]{:S(2)}) async-start(bf16[4,256,1536]{1,2,0:T(8,128)(2,1)} %bitcast.122), calls=%async_computation.3 | async-start | bytes 6291456 | tf_op jit(solution)/shard_map/all_to_all | solution.py:131
Sparse Core Ops, SparseCore 0:
  106.6 99.7 all-gather.7
  208.6 97.6 all-gather.5
where the time goes:
time: 424 us; the launch traced here: 422 us
  waiting for transfers between devices  144 us (34%)
  matrix products  89.2 us (21%)
  blocking collectives  63.9 us (15%)
  local copies, waits for them, and re-layouts  47.6 us (11%)
  other arithmetic  34.8 us (8%)
  starting transfers between devices  27 us (6%)
  between operations  14.9 us (4%)
    all_to_all x1, blocking collectives, local(): lax.all_to_all(key_rows, 'head', split_axis=1, concat_axis=0, tiled=True)  40.6 us
    all_to_all x1, waiting for transfers between devices, local(): lax.all_to_all(query_rows, 'head', split_axis=1, concat_axis=0, tiled=True)  35.2 us
    select_n x14, other arithmetic, lap(): jnp.where(position < mine, new, old)  33.7 us
    all_to_all x1, waiting for transfers between devices, local(): lax.all_to_all(grad_out, 'head', split_axis=1, concat_axis=0, tiled=True)  32.4 us
    all_to_all x1, waiting for transfers between devices, local(): lax.all_to_all(value_rows, 'head', split_axis=1, concat_axis=0, tiled=True)  32.2 us
    all_to_all x1, waiting for transfers between devices, local(): lax.all_to_all(query_gradient.reshape(flat_shape).astype(jnp.bfloat16), '...  27.6 us
    unnamed x1, blocking collectives  23.3 us
    unnamed x18, local copies, waits for them, and re-layouts  15.8 us
  transfers between devices with their start and end apart: 8, of which 6 were waited for; matrix products, arithmetic and copies ran while one was open for 35% of the time, Pallas kernels for 0%

commit v1 on v0

--- a/solution.py
+++ b/solution.py
@@ -127,14 +127,17 @@
         "njhd,nhde->njhe", key_block_list, state_after_bfloat, preferred_element_type=jnp.float32
     )
     flat_shape = (rows, heads_here * DH)
+    take_plane = lambda inner_x, axis_tag: jnp.concatenate(
+        lax.all_to_all(
+            jnp.stack(jnp.split(inner_x, lax.axis_size(axis_tag), axis=0)),
+            axis_name=axis_tag,
+            split_axis=0,
+            concat_axis=0,
+        ),
+        axis=1,
+    )
     return (
-        lax.all_to_all(
-            query_gradient.reshape(flat_shape).astype(jnp.bfloat16),
-            "head",
-            split_axis=0,
-            concat_axis=1,
-            tiled=True,
-        ),
+        take_plane(query_gradient.reshape(flat_shape).astype(jnp.bfloat16), "head"),
         lax.all_to_all(
             grad_key.reshape(flat_shape).astype(jnp.bfloat16),
             "head",

time: 424 us -> 423 us (level)
  no operation moved by 1% of the time
where the time goes in v1:
time: 423 us; the launch traced here: 422 us
  waiting for transfers between devices  144 us (34%)
  matrix products  87.5 us (21%)
  blocking collectives  63.9 us (15%)
  local copies, waits for them, and re-layouts  47.8 us (11%)
  other arithmetic  36.6 us (9%)
  starting transfers between devices  27 us (6%)
  between operations  14.9 us (4%)
    all_to_all x1, blocking collectives, local(): lax.all_to_all(key_rows, 'head', split_axis=1, concat_axis=0, tiled=True)  40.6 us
    all_to_all x1, waiting for transfers between devices, local(): lax.all_to_all(query_rows, 'head', split_axis=1, concat_axis=0, tiled=True)  35.2 us
    select_n x14, other arithmetic, lap(): jnp.where(position < mine, new, old)  33.7 us
    all_to_all x1, waiting for transfers between devices, local(): lax.all_to_all(grad_out, 'head', split_axis=1, concat_axis=0, tiled=True)  32.4 us
    all_to_all x1, waiting for transfers between devices, local(): lax.all_to_all(value_rows, 'head', split_axis=1, concat_axis=0, tiled=True)  32.2 us
    all_to_all x1, waiting for transfers between devices, local(): lax.all_to_all(jnp.stack(jnp.split(inner_x, lax.axis_size(axis_tag), axis...  27.6 us
    unnamed x1, blocking collectives  23.3 us
    unnamed x18, local copies, waits for them, and re-layouts  15.8 us
  transfers between devices with their start and end apart: 8, of which 6 were waited for; matrix products, arithmetic and copies ran while one was open for 35% of the time, Pallas kernels for 0%

profile of v1, /device:TPU:0, one launch (start us, length us, event | category | flops | bytes accessed | tf_op | source)
XLA Modules:
  0.0 421.6 jit_solution(17541238209569439025)
XLA Ops:
  7.2 4.6 %copy.37 = bf16[256,6144]{0,1:T(8,128)(2,1)} copy(bf16[256,6144]{1,0:T(8,128)(2,1)} %param.12) | data formatting | bytes 6291456 | tf_op args[3]
  11.8 4.3 %all-to-all-start = ((bf16[256,4,1536]{0,2,1:T(8,128)(2,1)}), bf16[256,4,1536]{0,2,1:T(8,128)(2,1)S(1)}, u32[]{:S(2)}, u32[]{:S(2)}) async-start(bf16[256,4,1536]{0,2,1:T(8,128)(2,1)} %bitcast.128), calls=%async_computation | async-start | bytes 6291456 | tf_op jit(solution)/shard_map/all_to_all | solution.py:39
  16.1 4.6 %copy.75 = bf16[256,6144]{0,1:T(8,128)(2,1)} copy(bf16[256,6144]{1,0:T(8,128)(2,1)} %param.9) | data formatting | bytes 6291456 | tf_op jit(solution)/shard_map/all_to_all | solution.py:36
  20.7 32.4 %all-to-all-done = bf16[256,4,1536]{0,2,1:T(8,128)(2,1)S(1)} async-done(((bf16[256,4,1536]{0,2,1:T(8,128)(2,1)}), bf16[256,4,1536]{0,2,1:T(8,128)(2,1)S(1)}, u32[]{:S(2)}, u32[]{:S(2)}) %all-to-all-start) | async-done | bytes 3145760 | tf_op jit(solution)/shard_map/all_to_all | solution.py:39
  53.1 4.8 %all-to-all-start.4 = ((bf16[256,4,1536]{0,2,1:T(8,128)(2,1)}), bf16[256,4,1536]{0,2,1:T(8,128)(2,1)}, u32[]{:S(2)}, u32[]{:S(2)}) async-start(bf16[256,4,1536]{0,2,1:T(8,128)(2,1)} %bitcast.125), calls=%async_computation.4 | async-start | bytes 6291456 | tf_op jit(solution)/shard_map/all_to_all | solution.py:36
  57.9 0.6 dynamic-slice
  59.2 0.2 exponential_dynamic-update-slice_fusion
  59.4 0.1 fusion.55
  59.5 0.1 multiply_exponential_fusion
  59.6 35.2 %all-to-all-done.4 = bf16[256,4,1536]{0,2,1:T(8,128)(2,1)} async-done(((bf16[256,4,1536]{0,2,1:T(8,128)(2,1)}), bf16[256,4,1536]{0,2,1:T(8,128)(2,1)}, u32[]{:S(2)}, u32[]{:S(2)}) %all-to-all-start.4) | async-done | bytes 3145760 | tf_op jit(solution)/shard_map/all_to_all | solution.py:36
  94.8 2.9 fusion.13
  97.7 1.7 copy-done.4
  99.4 7.1 %fusion.16 = f32[12,1,128,128]{3,1,2,0:T(1,128)} fusion(f32[4,12,128,128]{3,2,1,0:T(8,128)S(1)} %fusion.13, f32[12,4,1,1]{1,0,2,3:T(8,128)S(1)} %get-tuple-element.257), kind=kOutput, calls=%fused_computation.30 | convolution fusion | flops 9437184 | bytes 3932352 | tf_op jit(solution)/shard_map/hm,mhde->hde/dot_general | solution.py:93
  106.5 4.6 %copy.38 = bf16[256,6144]{0,1:T(8,128)(2,1)} copy(bf16[256,6144]{1,0:T(8,128)(2,1)} %param.11) | data formatting | bytes 6291456 | tf_op args[2]
  111.1 4.7 %all-to-all-start.1 = ((bf16[256,4,1536]{0,2,1:T(8,128)(2,1)}), bf16[256,4,1536]{0,2,1:T(8,128)(2,1)}, u32[]{:S(2)}, u32[]{:S(2)}) async-start(bf16[256,4,1536]{0,2,1:T(8,128)(2,1)} %bitcast.127), calls=%async_computation.1 | async-start | bytes 6291456 | tf_op jit(solution)/shard_map/all_to_all | solution.py:38
  115.8 4.7 %copy.73 = bf16[256,6144]{0,1:T(8,128)(2,1)} copy(bf16[256,6144]{1,0:T(8,128)(2,1)} %param.10) | data formatting | bytes 6291456 | tf_op jit(solution)/shard_map/all_to_all | solution.py:37
  120.5 32.2 %all-to-all-done.1 = bf16[256,4,1536]{0,2,1:T(8,128)(2,1)} async-done(((bf16[256,4,1536]{0,2,1:T(8,128)(2,1)}), bf16[256,4,1536]{0,2,1:T(8,128)(2,1)}, u32[]{:S(2)}, u32[]{:S(2)}) %all-to-all-start.1) | async-done | bytes 3145760 | tf_op jit(solution)/shard_map/all_to_all | solution.py:38
  152.7 40.6 %all_to_all.101 = bf16[256,4,1536]{0,2,1:T(8,128)(2,1)S(1)} all-to-all(bf16[256,4,1536]{0,2,1:T(8,128)(2,1)} %bitcast.129), channel_id=1, replica_groups=mesh['ctx'=8,'head'=4] {'head'}, dimensions={1} | all-to-all | bytes 6291456 | tf_op jit(solution)/shard_map/all_to_all | solution.py:37
  193.3 4.0 fusion.12
  197.4 1.7 copy-done.3
  199.0 7.1 %fusion.20 = f32[12,1,128,128]{3,1,2,0:T(1,128)} fusion(f32[4,12,128,128]{3,2,1,0:T(8,128)S(1)} %fusion.12, f32[12,4,1,1]{1,0,2,3:T(8,128)S(1)} %get-tuple-element.259), kind=kOutput, calls=%fused_computation.34 | convolution fusion | flops 9437184 | bytes 3932352 | tf_op jit(solution)/shard_map/hm,mhde->hde/dot_general | solution.py:92
  206.1 23.3 %all-reduce = f32[96]{0:T(128)S(1)} all-reduce(f32[96]{0:T(128)S(1)} %get-tuple-element.249), channel_id=2, replica_groups=mesh['ctx'=8,'head'=4] {'ctx'}, use_global_device_ids=true, to_apply=%add | all-reduce | flops 96 | bytes 768
  229.5 0.1 reshape.278
  229.6 0.1 fusion.36
  229.7 0.5 exponential_select_fusion
  230.2 4.9 %multiply_convert_fusion.1 = bf16[4,12,256,256]{3,2,1,0:T(8,128)(2,1)S(1)} fusion(f32[12,256,256]{2,1,0:T(8,128)S(1)} %exponential_select_fusion, bf16[4,256,12,128]{1,3,2,0:T(8,128)(2,1)S(1)} %bitcast.117, bf16[4,256,12,128]{1,3,2,0:T(8,128)(2,1)} %bitcast.5), kind=kOutput, calls=%fused_computation.7 | convolution fusion | flops 811597824 | bytes 15728640 | tf_op jit(solution)/shard_map/nihd,njhd->nhij/dot_general | solution.py:57
  235.1 2.6 copy-done.1
  237.7 5.5 %fusion.63 = f32[4,12,256,128]{2,3,1,0:T(8,128)} fusion(bf16[4,256,12,128]{1,3,2,0:T(8,128)(2,1)} %bitcast.30, bf16[4,12,256,256]{3,2,1,0:T(8,128)(2,1)S(1)} %multiply_convert_fusion.1), kind=kOutput, calls=%fused_computation.86 | convolution fusion | flops 805306368 | bytes 15728640 | tf_op jit(solution)/shard_map/nhij,nihd->njhd/dot_general | solution.py:116
  243.2 6.2 %rev.7 = f32[8,12,128,128]{3,2,1,0:T(8,128)} reverse(f32[8,12,128,128]{3,2,1,0:T(8,128)} %bitcast.131), dimensions={0} | reverse | bytes 12582912 | tf_op jit(solution)/shard_map/rev | solution.py:15
  249.5 16.9 %while.29 = (s32[]{:T(128)}, f32[12,128,128]{2,1,0:T(8,128)}, s32[]{:T(128)}, f32[8,12]{1,0:T(8,128)S(1)}, f32[8,12,128,128]{3,2,1,0:T(8,128)}, /*index=5*/s32[]{:T(128)}, s32[]{:T(128)}) while((s32[]{:T(128)}, f32[12,128,128]{2,1,0:T(8,128)}, s32[]{:T(128)}, f32[8,12]{1,0:T(8,128)S(1)}, f32[8,12,128,128]{3,2,1,0:T(8,128)}, ...), condition=%wide.region_3.4_spmd.clone, body=%wide.region_2.3_spmd.clone.sunk | while | flops 786436 | bytes 2359545 | solution.py:25
  249.5 2.4 fusion.83
  251.9 2.4 fusion.83
  254.3 2.4 fusion.83
  256.7 2.4 fusion.83
  259.1 2.4 fusion.83
  261.5 2.4 fusion.83
  264.0 2.4 fusion.83
  266.4 10.8 %fusion.32 = bf16[4,12,128,128]{3,0,2,1:T(4,128)(2,1)} fusion(f32[12,4]{1,0:T(8,128)S(1)} %get-tuple-element.260, f32[12,128,128]{2,1,0:T(8,128)} %get-tuple-element.192, f32[4,12,128,128]{3,2,1,0:T(8,128)} %copy-done.4, f32[4,4]{1,0:T(4,128)S(1)} %add_maximum_fusion, f32[12]{0:T(128)S(1)} %broadcast_multiply_fusion, pred[4,4]{1,0:T(4,128)(4,1)S(1)} %fusion.57), kind=kOutput, calls=%fused_computation.40 | convolution fusion | flops 40108416 | bytes 5505344 | tf_op jit(solution)/shard_map/hnm,mhde->nhde/dot_general | solution.py:101
  277.2 3.8 copy.55
  281.0 6.9 %fusion.6 = bf16[4,256,12,128]{1,3,2,0:T(8,128)(2,1)} fusion(f32[4,12,256,128]{2,3,1,0:T(8,128)} %fusion.63, f32[256,12]{0,1:T(8,128)S(1)} %get-tuple-element.262, bf16[4,12,128,128]{2,3,1,0:T(8,128)(2,1)} %copy.55, bf16[4,256,12,128]{1,3,2,0:T(8,128)(2,1)} %bitcast.5), kind=kOutput, calls=%fused_computation.14 | convolution fusion | flops 407371776 | bytes 14168064 | tf_op jit(solution)/shard_map/njhe,nhde->njhd/dot_general | solution.py:118
  287.9 4.9 %all-to-all-start.5 = ((bf16[4,256,1536]{1,2,0:T(8,128)(2,1)}), bf16[4,256,1536]{1,2,0:T(8,128)(2,1)}, u32[]{:S(2)}, u32[]{:S(2)}) async-start(bf16[4,256,1536]{1,2,0:T(8,128)(2,1)} %bitcast.130), calls=%async_computation.5 | async-start | bytes 6291456 | tf_op jit(solution)/shard_map/all_to_all | solution.py:141
  292.8 8.5 %fusion.62 = f32[4,12,256,128]{2,3,1,0:T(8,128)} fusion(bf16[4,12,256,256]{3,2,1,0:T(8,128)(2,1)} %copy-done.1, bf16[4,256,12,128]{1,3,2,0:T(8,128)(2,1)} %bitcast.121), kind=kOutput, calls=%fused_computation.85 | convolution fusion | flops 805306368 | bytes 15728640 | tf_op jit(solution)/shard_map/nhij,njhd->nihd/dot_general | solution.py:108
  301.3 9.1 %fusion.2 = f32[4,12,256,128]{2,3,1,0:T(8,128)} fusion(bf16[4,256,12,128]{1,3,2,0:T(8,128)(2,1)S(1)} %bitcast.118, f32[12,256,256]{2,1,0:T(8,128)} %copy-done.2, bf16[4,256,12,128]{1,3,2,0:T(8,128)(2,1)} %bitcast.30, bf16[4,256,12,128]{1,3,2,0:T(8,128)(2,1)} %bitcast.122), kind=kOutput, calls=%fused_computation.8 | convolution fusion | flops 1616904192 | bytes 18874368 | tf_op jit(solution)/shard_map/nhij,nihe->njhe/dot_general | solution.py:121
  310.3 6.9 %fusion.4 = bf16[4,256,12,128]{1,3,2,0:T(8,128)(2,1)} fusion(f32[4,12,256,128]{2,3,1,0:T(8,128)} %fusion.2, f32[256,12]{0,1:T(8,128)S(1)} %get-tuple-element.262, bf16[4,12,128,128]{2,3,1,0:T(8,128)(2,1)} %copy.55, bf16[4,256,12,128]{1,3,2,0:T(8,128)(2,1)} %bitcast.123), kind=kOutput, calls=%fused_computation.11 | convolution fusion | flops 407371776 | bytes 14168064 | tf_op jit(solution)/shard_map/njhd,nhde->njhe/dot_general | solution.py:126
  317.3 12.3 %all-to-all-done.5 = bf16[4,256,1536]{1,2,0:T(8,128)(2,1)} async-done(((bf16[4,256,1536]{1,2,0:T(8,128)(2,1)}), bf16[4,256,1536]{1,2,0:T(8,128)(2,1)}, u32[]{:S(2)}, u32[]{:S(2)}) %all-to-all-start.5) | async-done | bytes 3145760 | tf_op jit(solution)/shard_map/all_to_all | solution.py:141
  329.5 4.6 %all-to-all-start.6 = ((bf16[4,256,1536]{1,2,0:T(8,128)(2,1)}), bf16[4,256,1536]{1,2,0:T(8,128)(2,1)}, u32[]{:S(2)}, u32[]{:S(2)}) async-start(bf16[4,256,1536]{1,2,0:T(8,128)(2,1)} %bitcast.124), calls=%async_computation.6 | async-start | bytes 6291456 | tf_op jit(solution)/shard_map/all_to_all | solution.py:148
  334.2 16.9 %while.28 = (s32[]{:T(128)}, f32[12,128,128]{2,1,0:T(8,128)}, s32[]{:T(128)}, f32[8,12]{1,0:T(8,128)S(1)}, f32[8,12,128,128]{3,2,1,0:T(8,128)}, /*index=5*/s32[]{:T(128)}, s32[]{:T(128)}) while((s32[]{:T(128)}, f32[12,128,128]{2,1,0:T(8,128)}, s32[]{:T(128)}, f32[8,12]{1,0:T(8,128)S(1)}, f32[8,12,128,128]{3,2,1,0:T(8,128)}, ...), condition=%wide.region_1.2_spmd.clone, body=%wide.region_0.1_spmd.clone.sunk | while | flops 786436 | bytes 2359545 | solution.py:25
  334.2 2.2 fusion.82
  336.4 2.4 fusion.82
  338.9 2.4 fusion.82
  341.3 2.4 fusion.82
  343.8 2.4 fusion.82
  346.2 2.4 fusion.82
  348.7 2.4 fusion.82
  351.1 10.0 %fusion.29 = bf16[4,12,128,128]{3,0,2,1:T(4,128)(2,1)S(1)} fusion(f32[12,4]{1,0:T(8,128)S(1)} %get-tuple-element.258, f32[12,128,128]{2,1,0:T(8,128)} %get-tuple-element.191, f32[4,12,128,128]{3,2,1,0:T(8,128)} %copy-done.3, f32[4,4]{1,0:T(4,128)S(1)} %add_maximum_fusion.1, f32[12]{0:T(128)S(1)} %broadcast_multiply_fusion, pred[4,4]{1,0:T(4,128)(4,1)S(1)} %fusion.58), kind=kOutput, calls=%fused_computation.39 | convolution fusion | flops 40108416 | bytes 5505344 | tf_op jit(solution)/shard_map/hnm,mhde->nhde/dot_general | solution.py:98
  361.1 4.0 fusion.8
  365.0 0.2 fusion.61
  365.3 1.9 pad_maximum_fusion
  367.1 4.0 all-to-all-done.6
  371.1 3.7 all-to-all-start.3
  374.8 4.6 %copy.76 = bf16[256,6144]{1,0:T(8,128)(2,1)} copy(bf16[256,6144]{0,1:T(8,128)(2,1)} %bitcast.43) | data formatting | bytes 6291456 | tf_op jit(solution)/shard_map/all_to_all | solution.py:141
  379.5 4.6 %copy.77 = bf16[256,6144]{1,0:T(8,128)(2,1)} copy(bf16[256,6144]{0,1:T(8,128)(2,1)} %bitcast.48) | data formatting | bytes 6291456 | tf_op jit(solution)/shard_map/all_to_all | solution.py:148
  384.1 27.6 %all-to-all-done.3 = bf16[4,256,1536]{1,2,0:T(8,128)(2,1)S(1)} async-done(((bf16[4,256,1536]{1,2,0:T(8,128)(2,1)}), bf16[4,256,1536]{1,2,0:T(8,128)(2,1)S(1)}, u32[]{:S(2)}, u32[]{:S(2)}) %all-to-all-start.3) | async-done | bytes 3145760 | tf_op jit(solution)/shard_map/all_to_all | solution.py:131
  411.7 3.0 copy.74
  (44 shorter events, 0.4 us)
Async XLA Ops:
  11.8 41.3 %all-to-all-start = ((bf16[256,4,1536]{0,2,1:T(8,128)(2,1)}), bf16[256,4,1536]{0,2,1:T(8,128)(2,1)S(1)}, u32[]{:S(2)}, u32[]{:S(2)}) async-start(bf16[256,4,1536]{0,2,1:T(8,128)(2,1)} %bitcast.128), calls=%async_computation | async-start | bytes 6291456 | tf_op jit(solution)/shard_map/all_to_all | solution.py:39
  53.1 4.9 %copy-start.6 = (u32[32]{0:T(128)S(1)}, u32[32]{0:T(128)}, u32[]{:S(2)}) copy-start(u32[32]{0:T(128)} %constant.87) | copy-start | bytes 388
  53.1 6.1 %copy-start.5 = (f32[48]{0:T(128)S(1)}, f32[48]{0:T(128)}, u32[]{:S(2)}) copy-start(f32[48]{0:T(128)} %param.13) | copy-start | bytes 580
  53.1 41.8 %all-to-all-start.4 = ((bf16[256,4,1536]{0,2,1:T(8,128)(2,1)}), bf16[256,4,1536]{0,2,1:T(8,128)(2,1)}, u32[]{:S(2)}, u32[]{:S(2)}) async-start(bf16[256,4,1536]{0,2,1:T(8,128)(2,1)} %bitcast.125), calls=%async_computation.4 | async-start | bytes 6291456 | tf_op jit(solution)/shard_map/all_to_all | solution.py:36
  57.9 185.4 %all-gather.8.cloned.1.call-start = ((), (), s32[]{:S(2)}) async-start(), calls=%async_computation.8 | async-start | bytes 7077888 | tf_op jit(solution)/shard_map/all_gather | solution.py:13
  97.7 1.7 copy-start.4
  111.1 41.6 %all-to-all-start.1 = ((bf16[256,4,1536]{0,2,1:T(8,128)(2,1)}), bf16[256,4,1536]{0,2,1:T(8,128)(2,1)}, u32[]{:S(2)}, u32[]{:S(2)}) async-start(bf16[256,4,1536]{0,2,1:T(8,128)(2,1)} %bitcast.127), calls=%async_computation.1 | async-start | bytes 6291456 | tf_op jit(solution)/shard_map/all_to_all | solution.py:38
  115.8 218.4 %all-gather.6.cloned.1.call-start = ((), (), s32[]{:S(2)}) async-start(), calls=%async_computation.7 | async-start | bytes 7077888 | tf_op jit(solution)/shard_map/all_gather | solution.py:13
  193.3 4.1 copy-start
  197.4 1.7 copy-start.3
  230.2 4.9 %copy-start.2 = (f32[12,256,256]{2,1,0:T(8,128)}, f32[12,256,256]{2,1,0:T(8,128)S(1)}, u32[]{:S(2)}) copy-start(f32[12,256,256]{2,1,0:T(8,128)S(1)} %exponential_select_fusion) | copy-start | bytes 9437188
  235.1 2.6 copy-start.1
  287.9 41.6 %all-to-all-start.5 = ((bf16[4,256,1536]{1,2,0:T(8,128)(2,1)}), bf16[4,256,1536]{1,2,0:T(8,128)(2,1)}, u32[]{:S(2)}, u32[]{:S(2)}) async-start(bf16[4,256,1536]{1,2,0:T(8,128)(2,1)} %bitcast.130), calls=%async_computation.5 | async-start | bytes 6291456 | tf_op jit(solution)/shard_map/all_to_all | solution.py:141
  329.5 41.6 %all-to-all-start.6 = ((bf16[4,256,1536]{1,2,0:T(8,128)(2,1)}), bf16[4,256,1536]{1,2,0:T(8,128)(2,1)}, u32[]{:S(2)}, u32[]{:S(2)}) async-start(bf16[4,256,1536]{1,2,0:T(8,128)(2,1)} %bitcast.124), calls=%async_computation.6 | async-start | bytes 6291456 | tf_op jit(solution)/shard_map/all_to_all | solution.py:148
  371.1 40.6 %all-to-all-start.3 = ((bf16[4,256,1536]{1,2,0:T(8,128)(2,1)}), bf16[4,256,1536]{1,2,0:T(8,128)(2,1)S(1)}, u32[]{:S(2)}, u32[]{:S(2)}) async-start(bf16[4,256,1536]{1,2,0:T(8,128)(2,1)} %pad_maximum_fusion), calls=%async_computation.3 | async-start | bytes 6291456 | tf_op jit(solution)/shard_map/all_to_all | solution.py:131
Sparse Core Ops, SparseCore 0:
  106.6 99.7 all-gather.7
  208.6 97.6 all-gather.5
